TPU v7x, 32 devices: a whole 2x2x4 slice. The times are simulated.
32 devices in a mesh: row: 8 (over z, x), col: 4 (over y, core).
Axes of the slice: x: 2, y: 2, z: 4, core: 2. Of those that a mesh axis runs over, the one named last changes fastest.
Arguments:
- momentum: bfloat16 [16384, 16384], P('row', 'col'), may hold values from -16 to 16
- gradient: bfloat16 [16384, 16384], P('row', 'col'), may hold values from -6 to 6
- right_basis: bfloat16 [1024, 16384], P('row', 'col'), may hold values from -1 to 1
Outputs:
- momentum_next: bfloat16 [16384, 16384], P('row', 'col')
- basis_next: float32 [1024, 16384], P('row', 'col')
- update: bfloat16 [16384, 16384], P('row', 'col')
All inputs are finite; a program needn't handle non-finite values.
Results may differ from a plain program's by a relative error of at most 0.02.
Values may be sent and summed in bfloat16 or wider, within the bound.
A program may use at most 128 MiB of HBM per device.

v0:
```python
import math

import jax
import jax.numpy as jnp
from jax import lax
from jax.sharding import PartitionSpec as P

D = 16384
RANK = 1024


momentum_decay = 0.95
epsilon = 1e-06


def orthonormalize(projected, gram_matrix):
    lower_factor = jnp.linalg.cholesky(gram_matrix)
    solved = jax.scipy.linalg.solve_triangular(lower_factor, projected.T, lower=True)
    return solved.T.astype(jnp.bfloat16)


def self_gram(projected):
    return lax.dot_general(
        projected, projected, (((0,), (0,)), ((), ())), precision=lax.Precision.HIGHEST
    )


def body(momentum, gradient, right_basis):
    buffer = (momentum.astype(jnp.float32) + gradient.astype(jnp.float32)).astype(jnp.bfloat16)
    rank_rows = right_basis.shape[0]
    partial_value = lax.dot_general(
        buffer,
        lax.all_gather(right_basis, "row", axis=0, tiled=True),
        (((1,), (1,)), ((), ())),
        preferred_element_type=jnp.float32,
    )
    row_share = lax.psum_scatter(
        partial_value.astype(jnp.bfloat16), "col", scatter_dimension=0, tiled=True
    ).astype(jnp.float32)
    gram_matrix = lax.psum(self_gram(row_share), ("row", "col"))
    ortho_share = orthonormalize(row_share, gram_matrix)
    orthonormal = lax.all_gather(ortho_share, "col", axis=0, tiled=True)
    right_share = lax.psum_scatter(
        lax.dot_general(
            orthonormal, buffer, (((0,), (0,)), ((), ())), preferred_element_type=jnp.float32
        ).astype(jnp.bfloat16),
        "row",
        scatter_dimension=0,
        tiled=True,
    )
    right_wide = right_share.astype(jnp.float32)
    gathered = lax.all_gather(right_share, "row", axis=0, tiled=True)
    gathered_wide = gathered.astype(jnp.float32)
    sums_total = lax.psum(jnp.sum(gathered_wide * gathered_wide, axis=1), "col")
    inverse_norm = lax.rsqrt(sums_total + epsilon)[:, None]
    scaled = (gathered_wide * inverse_norm).astype(jnp.bfloat16)
    feedback = jnp.dot(orthonormal, gathered, preferred_element_type=jnp.float32)
    direction = jnp.dot(orthonormal, scaled, preferred_element_type=jnp.float32)
    offset = lax.axis_index("row") * rank_rows
    basis_next = right_wide * lax.dynamic_slice_in_dim(inverse_norm, offset, rank_rows, 0)
    momentum_next = (buffer.astype(jnp.float32) - (1.0 - momentum_decay) * feedback).astype(
        jnp.bfloat16
    )
    update_scale = D / math.sqrt(RANK)
    update = (update_scale * direction).astype(jnp.bfloat16)
    return (momentum_next, basis_next, update)


def solution(mesh):
    return jax.shard_map(
        body,
        mesh=mesh,
        in_specs=(P("row", "col"), P("row", "col"), P("row", "col")),
        out_specs=(P("row", "col"), P("row", "col"), P("row", "col")),
        check_vma=False,
    )
```

profile of v0, /device:TPU:0, one launch (start us, length us, event | category | flops | bytes accessed | tf_op | source)
XLA Modules:
  0.0 1132.3 jit_solution(6209591932826324028)
XLA Ops:
  7.9 129.4 %all-gather.4.cloned.1.call-done = bf16[1024,4096]{1,0:T(8,128)(2,1)} async-done(((bf16[128,4096]{1,0:T(8,128)(2,1)}), bf16[1024,4096]{1,0:T(8,128)(2,1)}) %all-gather.4.cloned.1.call-update) | async-done | bytes 8388624 | tf_op jit(solution)/shard_map/all_gather | solution.py:33
  137.3 25.8 %convolution_convert_fusion.1 = bf16[2048,1024]{1,0:T(8,128)(2,1)} fusion(bf16[1024,4096]{1,0:T(8,128)(2,1)} %all-gather.4.cloned.1.call-done, bf16[2048,4096]{1,0:T(8,128)(2,1)} %param.4, bf16[2048,4096]{1,0:T(8,128)(2,1)} %param.3), kind=kOutput, calls=%fused_computation.15 | convolution fusion | flops 17215520768 | bytes 46137344 | tf_op jit(solution)/shard_map/dot_general | solution.py:31
  163.2 42.9 %reduce-scatter.3.cloned.1.call-done = bf16[512,1024]{1,0:T(8,128)(2,1)} async-done(((bf16[2048,1024]{1,0:T(8,128)(2,1)}), bf16[512,1024]{1,0:T(8,128)(2,1)}) %reduce-scatter.3.cloned.1.call-update) | async-done | bytes 1048592 | tf_op jit(solution)/shard_map/reduce_scatter | solution.py:37
  206.1 4.9 fusion.67
  211.3 143.2 %all-reduce.3.cloned.1.call-done = f32[1024,1024]{0,1:T(8,128)} async-done(((f32[1024,1024]{0,1:T(8,128)}), f32[1024,1024]{0,1:T(8,128)}) %all-reduce.3.cloned.1.call-update) | async-done | bytes 4194320 | tf_op jit(solution)/shard_map/psum | solution.py:40
  354.5 5.5 copy.7
  360.0 4.4 fusion.4
  366.5 11.7 %cholesky.223 = f32[128,128]{1,0:T(8,128)S(1)} custom-call(f32[128,128]{1,0:T(8,128)S(1)} %cholesky.580), custom_call_target="Cholesky" | custom-call | tf_op jit(solution)/shard_map/jit(cholesky)/cholesky | solution.py:17
  378.2 9.8 custom-call.63
  388.1 2.5 cholesky.255
  395.2 12.1 %cholesky.244 = f32[128,128]{1,0:T(8,128)S(1)} custom-call(f32[128,128]{1,0:T(8,128)S(1)} %cholesky.584), custom_call_target="Cholesky" | custom-call | tf_op jit(solution)/shard_map/jit(cholesky)/cholesky | solution.py:17
  408.0 9.8 custom-call.64
  422.7 13.2 %cholesky.468 = f32[128,128]{1,0:T(8,128)} custom-call(f32[128,128]{1,0:T(8,128)} %cholesky.589), custom_call_target="Cholesky" | custom-call | tf_op jit(solution)/shard_map/jit(cholesky)/cholesky | solution.py:17
  438.0 11.3 custom-call.65
  451.2 2.3 convolution_subtract_fusion.2
  453.6 12.5 %cholesky.487 = f32[128,128]{1,0:T(8,128)} custom-call(f32[128,128]{1,0:T(8,128)S(1)} %cholesky.594), custom_call_target="Cholesky" | custom-call | tf_op jit(solution)/shard_map/jit(cholesky)/cholesky | solution.py:17
  468.2 10.4 custom-call.66
  482.9 11.7 %cholesky.506 = f32[128,128]{1,0:T(8,128)S(1)} custom-call(f32[128,128]{1,0:T(8,128)S(1)} %cholesky.599), custom_call_target="Cholesky" | custom-call | tf_op jit(solution)/shard_map/jit(cholesky)/cholesky | solution.py:17
  495.9 10.0 custom-call.67
  509.2 11.7 %cholesky.526 = f32[128,128]{1,0:T(8,128)S(1)} custom-call(f32[128,128]{1,0:T(8,128)S(1)} %cholesky.604), custom_call_target="Cholesky" | custom-call | tf_op jit(solution)/shard_map/jit(cholesky)/cholesky | solution.py:17
  522.2 9.8 custom-call.68
  535.0 12.0 %cholesky.546 = f32[128,128]{1,0:T(8,128)S(1)} custom-call(f32[128,128]{1,0:T(8,128)S(1)} %cholesky.609), custom_call_target="Cholesky" | custom-call | tf_op jit(solution)/shard_map/jit(cholesky)/cholesky | solution.py:17
  548.4 9.8 custom-call.69
  560.9 11.7 %cholesky.564 = f32[128,128]{1,0:T(8,128)S(1)} custom-call(f32[128,128]{1,0:T(8,128)S(1)} %convolution_subtract_fusion.13), custom_call_target="Cholesky" | custom-call | tf_op jit(solution)/shard_map/jit(cholesky)/cholesky | solution.py:17
  579.5 4.9 select_select_fusion
  584.4 29.0 %while.1 = (s32[]{:T(128)}, f32[1024,1024]{1,0:T(8,128)}, s32[8,2]{0,1:T(2,128)S(1)}, f32[8,128,128]{2,1,0:T(8,128)}, s32[]{:T(128)}) while((s32[]{:T(128)}, f32[1024,1024]{1,0:T(8,128)}, s32[8,2]{0,1:T(2,128)S(1)}, f32[8,128,128]{2,1,0:T(8,128)}, s32[]{:T(128)}) %tuple.57), condition=%wide.while_cond, body=%wide.while_body.sunk | while | flops 2 | bytes 132205 | solution.py:18
  585.1 3.0 bitcast_dynamic-update-slice_fusion.2
  588.7 3.0 bitcast_dynamic-update-slice_fusion.2
  592.3 3.0 bitcast_dynamic-update-slice_fusion.2
  596.0 3.0 bitcast_dynamic-update-slice_fusion.2
  599.6 3.0 bitcast_dynamic-update-slice_fusion.2
  603.2 3.0 bitcast_dynamic-update-slice_fusion.2
  606.9 3.0 bitcast_dynamic-update-slice_fusion.2
  610.5 2.9 bitcast_dynamic-update-slice_fusion.2
  613.4 80.2 %custom-call.70 = f32[8,128,128]{1,2,0:T(8,128)} custom-call(f32[8,128,128]{2,1,0:T(8,128)} %get-tuple-element.10), custom_call_target="InvertDiagBlocksLowerTriangular" | custom-call | tf_op jit(solution)/shard_map/jit(_solve_triangular)/triangular_solve | solution.py:18
  702.0 2.4 convolution_subtract_fusion.8
  705.4 2.8 convolution_subtract_fusion.9
  709.7 3.2 convolution_subtract_fusion.4
  714.0 3.6 convolution_subtract_fusion.7
  718.8 4.3 convolution_subtract_fusion.3
  724.2 33.9 %all-gather.6.cloned.1.call-done = bf16[2048,1024]{0,1:T(8,128)(2,1)} async-done(((bf16[512,1024]{0,1:T(8,128)(2,1)}), bf16[2048,1024]{0,1:T(8,128)(2,1)}) %all-gather.6.cloned.1.call-update) | async-done | bytes 4194320 | tf_op jit(solution)/shard_map/all_gather | solution.py:42
  758.1 24.2 %convolution_convert_fusion = bf16[1024,4096]{1,0:T(8,128)(2,1)} fusion(bf16[2048,1024]{0,1:T(8,128)(2,1)} %all-gather.6.cloned.1.call-done, bf16[2048,4096]{1,0:T(8,128)(2,1)} %param.4, bf16[2048,4096]{1,0:T(8,128)(2,1)} %param.3), kind=kOutput, calls=%fused_computation.10 | convolution fusion | flops 17217617920 | bytes 46137344 | tf_op jit(solution)/shard_map/dot_general | solution.py:44
  782.3 147.5 %reduce-scatter.5.cloned.1.call-done = bf16[128,4096]{1,0:T(8,128)(2,1)} async-done(((bf16[1024,4096]{1,0:T(8,128)(2,1)}), bf16[128,4096]{1,0:T(8,128)(2,1)}) %reduce-scatter.5.cloned.1.call-update) | async-done | bytes 1048592 | tf_op jit(solution)/shard_map/reduce_scatter | solution.py:43
  929.9 125.6 %all-gather.8.cloned.1.call-done = bf16[1024,4096]{1,0:T(8,128)(2,1)} async-done(((bf16[128,4096]{1,0:T(8,128)(2,1)}), bf16[1024,4096]{1,0:T(8,128)(2,1)}) %all-gather.8.cloned.1.call-update) | async-done | bytes 8388624 | tf_op jit(solution)/shard_map/all_gather | solution.py:52
  1055.5 5.1 fusion
  1060.5 5.9 psum.15
  1066.5 26.4 %multiply_convert_fusion = bf16[2048,4096]{1,0:T(8,128)(2,1)} fusion(bf16[2048,1024]{0,1:T(8,128)(2,1)} %all-gather.6.cloned.1.call-done, bf16[1024,4096]{1,0:T(8,128)(2,1)} %all-gather.8.cloned.1.call-done, f32[1024]{0:T(1024)S(1)} %add_rsqrt_fusion), kind=kOutput, calls=%fused_computation.2 | convolution fusion | flops 17209229312 | bytes 29364224 | tf_op jit(solution)/shard_map/dot_general | solution.py:58
  1092.9 30.5 %subtract_convert_fusion = bf16[2048,4096]{1,0:T(8,128)(2,1)} fusion(bf16[2048,1024]{0,1:T(8,128)(2,1)S(1)} %copy-done.5, bf16[1024,4096]{1,0:T(8,128)(2,1)} %all-gather.8.cloned.1.call-done, bf16[2048,4096]{1,0:T(8,128)(2,1)} %param.4, bf16[2048,4096]{1,0:T(8,128)(2,1)} %param.3), kind=kOutput, calls=%fused_computation.3 | convolution fusion | flops 17246978048 | bytes 62914560 | tf_op jit(solution)/shard_map/dot_general | solution.py:57
  (99 shorter events, 59.9 us)
Async XLA Ops:
  7.2 130.2 %all-gather.4.cloned.1.call-start = ((), (), s32[]{:S(2)}) async-start(), calls=%async_computation.2 | async-start | bytes 9437184 | tf_op jit(solution)/shard_map/all_gather | solution.py:33
  7.9 198.2 %reduce-scatter.3.cloned.1.call-start = ((), (), s32[]{:S(2)}) async-start(), calls=%async_computation.3 | async-start | bytes 5242880 | tf_op jit(solution)/shard_map/reduce_scatter | solution.py:37
  163.1 191.4 %all-reduce.3.cloned.1.call-start = ((), (), s32[]{:S(2)}) async-start(), calls=%async_computation.4 | async-start | bytes 8388608 | tf_op jit(solution)/shard_map/psum | solution.py:40
  206.1 5.0 copy-start
  211.0 547.1 %all-gather.6.cloned.1.call-start = ((), (), s32[]{:S(2)}) async-start(), calls=%async_computation.5 | async-start | bytes 5242880 | tf_op jit(solution)/shard_map/all_gather | solution.py:42
  364.5 2.0 copy-start.1
  394.5 0.8 copy-start.3
  693.6 7.2 copy-start.4
  724.2 205.7 %reduce-scatter.5.cloned.1.call-start = ((), (), s32[]{:S(2)}) async-start(), calls=%async_computation.6 | async-start | bytes 9437184 | tf_op jit(solution)/shard_map/reduce_scatter | solution.py:43
  782.3 273.2 %all-gather.8.cloned.1.call-start = ((), (), s32[]{:S(2)}) async-start(), calls=%async_computation.7 | async-start | bytes 9437184 | tf_op jit(solution)/shard_map/all_gather | solution.py:52
  1066.5 26.4 %copy-start.5 = (bf16[2048,1024]{0,1:T(8,128)(2,1)S(1)}, bf16[2048,1024]{0,1:T(8,128)(2,1)}, u32[]{:S(2)}) copy-start(bf16[2048,1024]{0,1:T(8,128)(2,1)} %all-gather.6.cloned.1.call-done) | copy-start | bytes 12582916
  1092.9 30.5 %copy-start.2 = (bf16[128,4096]{1,0:T(8,128)(2,1)S(1)}, bf16[128,4096]{1,0:T(8,128)(2,1)}, u32[]{:S(2)}) copy-start(bf16[128,4096]{1,0:T(8,128)(2,1)} %reduce-scatter.5.cloned.1.call-done) | copy-start | bytes 3145732
Sparse Core Ops, SparseCore 0:
  10.1 127.1 all-gather.3
  163.3 42.7 reduce-scatter.2
  212.2 142.2 all-reduce.2
  724.3 33.7 all-gather.5
  782.4 147.4 reduce-scatter.4
  931.9 123.5 all-gather.7
where the time goes:
time: 1140 us; the launch traced here: 1130 us
  waiting for transfers between devices  623 us (55%)
  other arithmetic  275 us (24%)
  matrix products  167 us (15%)
  local copies, waits for them, and re-layouts  41.1 us (4%)
  between operations  19.9 us (2%)
    another operation x30, other arithmetic, orthonormalize(): lower_factor = jnp.linalg.cholesky(gram_matrix)  178 us
    reduce_scatter x1, waiting for transfers between devices, body(): lax.psum_scatter(lax.dot_general(orthonormal, buffer, (((0,), (0,)), ((),...  148 us
    psum x1, waiting for transfers between devices, body(): gram_matrix = lax.psum(self_gram(row_share), ('row', 'col'))  143 us
    all_gather x1, waiting for transfers between devices, body(): lax.all_gather(right_basis, 'row', axis=0, tiled=True)  129 us
    all_gather x1, waiting for transfers between devices, body(): gathered = lax.all_gather(right_share, 'row', axis=0, tiled=True)  126 us
    another operation x3, other arithmetic, orthonormalize(): jax.scipy.linalg.solve_triangular(lower_factor, projected.T, lower=True)  85.1 us
    reduce_scatter x1, waiting for transfers between devices, body(): lax.psum_scatter(partial_value.astype(jnp.bfloat16), 'col', scatter_dimen...  42.9 us
    all_gather x1, waiting for transfers between devices, body(): orthonormal = lax.all_gather(ortho_share, 'col', axis=0, tiled=True)  33.9 us
  transfers between devices with their start and end apart: 6, of which 6 were waited for; matrix products, arithmetic and copies ran while one was open for 0% of the time, Pallas kernels for 0%

commit v1 on v0

v1 whole, which is shorter than its diff:
```python
import functools
import math

import jax
import jax.numpy as jnp
from jax import lax
from jax.experimental import pallas as pl
from jax.experimental.pallas import tpu as pltpu
from jax.sharding import PartitionSpec as P

D = 16384
RANK = 1024

momentum_decay = 0.95
epsilon = 1e-06

BLOCK = 128
GROUP = 8
PACK = 256
CHUNKS = 4

HIGHEST = lax.Precision.HIGHEST


def across(x, column):
    return jnp.broadcast_to(x[:, column : column + 1], (x.shape[0], BLOCK))


def down(x, row):
    return jnp.broadcast_to(x[row : row + 1, :], (GROUP, BLOCK))


def factor_block(block):
    groups = BLOCK // GROUP
    sub = lax.broadcasted_iota(jnp.int32, (GROUP, BLOCK), 0)
    lane = lax.broadcasted_iota(jnp.int32, (GROUP, BLOCK), 1)
    left = [block[GROUP * g : GROUP * (g + 1), :] for g in range(groups)]
    right = [jnp.where(lane == sub + GROUP * g, 1.0, 0.0) for g in range(groups)]
    inverse = []
    for g in range(groups):
        first = GROUP * g
        jordan_left, jordan_right = left[g], right[g]
        columns = [across(jordan_left, first + l) for l in range(GROUP)]
        forward_right, pivots = jordan_right, jnp.ones_like(jordan_left)
        for l in range(GROUP):
            pivot = down(columns[l], l)
            reciprocal = 1.0 / pivot
            mine = sub == l
            column = columns[l]
            row_left, row_right = down(jordan_left, l), down(jordan_right, l)
            forward_right = jnp.where(mine, row_right, forward_right)
            pivots = jnp.where(mine, pivot, pivots)
            row_left, row_right = row_left * reciprocal, row_right * reciprocal
            jordan_left = jnp.where(mine, row_left, jordan_left - column * row_left)
            jordan_right = jnp.where(mine, row_right, jordan_right - column * row_right)
            for m in range(l + 1, GROUP):
                row = down(columns[m], l) * reciprocal
                columns[m] = jnp.where(mine, row, columns[m] - column * row)
        inverse.append(forward_right * lax.rsqrt(pivots))
        rows_left = [down(jordan_left, l) for l in range(GROUP)]
        rows_right = [down(jordan_right, l) for l in range(GROUP)]
        for h in range(g + 1, groups):
            base = left[h]
            new_left, new_right = base, right[h]
            for l in range(GROUP):
                coefficient = across(base, first + l)
                new_left = new_left - coefficient * rows_left[l]
                new_right = new_right - coefficient * rows_right[l]
            left[h], right[h] = new_left, new_right
    return jnp.concatenate(inverse, axis=0)


def factor_kernel(packed_ref, share_ref, ortho_ref, work):
    rank = work.shape[0]
    blocks = rank // BLOCK
    offset = 0
    for i in range(rank // PACK):
        for j in range(i + 1):
            tile = packed_ref[:, offset : offset + PACK]
            offset += PACK
            work[PACK * i : PACK * (i + 1), PACK * j : PACK * (j + 1)] = tile
            if j < i:
                work[PACK * j : PACK * (j + 1), PACK * i : PACK * (i + 1)] = tile.T
    column_block = lax.broadcasted_iota(jnp.int32, (BLOCK, rank), 1) // BLOCK

    def step(k, carry):
        here = pl.ds(pl.multiple_of(k * BLOCK, BLOCK), BLOCK)
        x = factor_block(work[here, here])
        pivot_rows = jnp.dot(x, work[here, :], precision=HIGHEST, preferred_element_type=jnp.float32)
        wide = jnp.concatenate([x] * blocks, axis=1)
        pivot_rows = jnp.where(column_block == k, wide, pivot_rows)
        work[here, :] = pivot_rows

        def below(i, carry):
            there = pl.ds(pl.multiple_of(i * BLOCK, BLOCK), BLOCK)
            panel = lax.dot_general(
                work[there, here], x, (((1,), (1,)), ((), ())),
                precision=HIGHEST, preferred_element_type=jnp.float32,
            )
            work[there, here] = jnp.zeros((BLOCK, BLOCK), jnp.float32)
            work[there, :] = work[there, :] - jnp.dot(
                panel, work[here, :], precision=HIGHEST, preferred_element_type=jnp.float32
            )
            return carry

        lax.fori_loop(k + 1, blocks, below, 0)
        rest = jnp.where(column_block <= k, pivot_rows, 0.0)
        total = jnp.zeros((share_ref.shape[0], BLOCK), jnp.float32)
        for _ in range(3):
            part = rest.astype(jnp.bfloat16)
            rest = rest - part.astype(jnp.float32)
            total = total + lax.dot_general(
                share_ref[...], part, (((1,), (1,)), ((), ())),
                preferred_element_type=jnp.float32,
            )
        ortho_ref[:, here] = total.astype(jnp.bfloat16)
        return carry

    lax.fori_loop(0, blocks, step, 0)


def orthonormalize(row_share, packed):
    rank = row_share.shape[1]
    return pl.pallas_call(
        factor_kernel,
        out_shape=jax.ShapeDtypeStruct(row_share.shape, jnp.bfloat16),
        in_specs=[pl.BlockSpec(memory_space=pltpu.VMEM)] * 2,
        out_specs=pl.BlockSpec(memory_space=pltpu.VMEM),
        scratch_shapes=[pltpu.VMEM((rank, rank), jnp.float32)],
        compiler_params=pltpu.CompilerParams(vmem_limit_bytes=40 * 1024 * 1024),
        name="factor",
    )(packed, row_share)


def packed_gram(share):
    pieces = []
    for i in range(share.shape[1] // PACK):
        pieces.append(
            lax.dot_general(
                share[:, PACK * i : PACK * (i + 1)],
                share[:, : PACK * (i + 1)],
                (((0,), (0,)), ((), ())),
                preferred_element_type=jnp.float32,
            )
        )
    return jnp.concatenate(pieces, axis=1)


def body(momentum, gradient, right_basis):
    buffer = (momentum.astype(jnp.float32) + gradient.astype(jnp.float32)).astype(jnp.bfloat16)
    rank_rows = right_basis.shape[0]
    partial_value = lax.dot_general(
        buffer,
        lax.all_gather(right_basis, "row", axis=0, tiled=True),
        (((1,), (1,)), ((), ())),
        preferred_element_type=jnp.float32,
    )
    row_share = lax.psum_scatter(
        partial_value.astype(jnp.bfloat16), "col", scatter_dimension=0, tiled=True
    )
    packed = lax.psum(packed_gram(row_share), ("row", "col"))
    ortho_share = orthonormalize(row_share, packed)
    orthonormal = lax.all_gather(ortho_share, "col", axis=0, tiled=True)
    width = buffer.shape[1] // CHUNKS
    shares, gathered, sums, feedback = [], [], [], []
    for c in range(CHUNKS):
        part = buffer[:, c * width : (c + 1) * width]
        shares.append(
            lax.psum_scatter(
                lax.dot_general(
                    orthonormal, part, (((0,), (0,)), ((), ())),
                    preferred_element_type=jnp.float32,
                ).astype(jnp.bfloat16),
                "row",
                scatter_dimension=0,
                tiled=True,
            )
        )
    for c in range(CHUNKS):
        gathered.append(lax.all_gather(shares[c], "row", axis=0, tiled=True))
        wide = gathered[c].astype(jnp.float32)
        sums.append(jnp.sum(wide * wide, axis=1))
        product = jnp.dot(orthonormal, gathered[c], preferred_element_type=jnp.float32)
        part = buffer[:, c * width : (c + 1) * width]
        feedback.append(
            (part.astype(jnp.float32) - (1.0 - momentum_decay) * product).astype(jnp.bfloat16)
        )
    momentum_next = jnp.concatenate(feedback, axis=1)
    sums_total = lax.psum(functools.reduce(jnp.add, sums), "col")
    inverse_norm = lax.rsqrt(sums_total + epsilon)[:, None]
    offset = lax.axis_index("row") * rank_rows
    mine = lax.dynamic_slice_in_dim(inverse_norm, offset, rank_rows, 0)
    basis_next = jnp.concatenate([s.astype(jnp.float32) * mine for s in shares], axis=1)
    whole = jnp.concatenate(gathered, axis=1)
    scaled = (whole.astype(jnp.float32) * inverse_norm).astype(jnp.bfloat16)
    direction = jnp.dot(orthonormal, scaled, preferred_element_type=jnp.float32)
    update_scale = D / math.sqrt(RANK)
    update = (update_scale * direction).astype(jnp.bfloat16)
    return (momentum_next, basis_next, update)


def solution(mesh):
    return jax.shard_map(
        body,
        mesh=mesh,
        in_specs=(P("row", "col"), P("row", "col"), P("row", "col")),
        out_specs=(P("row", "col"), P("row", "col"), P("row", "col")),
        check_vma=False,
    )
```

time: 1140 us -> 1070 us (0.939)
  other arithmetic: 275 us -> 44.6 us
  waiting for transfers between devices: 623 us -> 723 us
  Pallas kernels: 0 us -> 73.5 us
  matrix products: 167 us -> 133 us
  local copies, waits for them, and re-layouts: 41.1 us -> 68.2 us
    another operation x33 -> x0, other arithmetic: 263 us -> none  [the longest x30 178 us: orthonormalize(): lower_factor = jnp.linalg.cholesky(gram_matrix)]
    reduce_scatter x1 -> x4, waiting for transfers between devices: 148 us -> 252 us  [body(): lax.psum_scatter(lax.dot_general(orthonormal, part, (((0,), (0,)), ((), (...]
    pallas_call x0 -> x1, Pallas kernels: none -> 73.5 us  [orthonormalize(): pl.pallas_call(factor_kernel, out_shape=jax.ShapeDtypeStruct(row_share.sh...]
    all_gather x1 -> x4, waiting for transfers between devices: 126 us -> 193 us  [body(): gathered.append(lax.all_gather(shares[c], 'row', axis=0, tiled=True))]
    all_gather x1, waiting for transfers between devices: 129 us -> 64.1 us  [body(): lax.all_gather(right_basis, 'row', axis=0, tiled=True)]
    unnamed x18 -> x25, local copies, waits for them, and re-layouts: 3.26 us -> 68.1 us
    another operation x29 -> x0, matrix products: 55.5 us -> none  [the longest x15 29.9 us: orthonormalize(): jax.scipy.linalg.solve_triangular(lower_factor, projected.T, lower=True)]
    another operation x35 -> x1, local copies, waits for them, and re-layouts: 32.3 us -> 0.07 us
  transfers between devices with their start and end apart: 6 -> 12, of which waited for: 6 -> 12; matrix products, arithmetic and copies ran while one was open for 0% -> 9% of each run, Pallas kernels for 0% -> 0%
where the time goes in v1:
time: 1070 us; the launch traced here: 1060 us
  waiting for transfers between devices  723 us (68%)
  matrix products  133 us (12%)
  Pallas kernels  73.5 us (7%)
  local copies, waits for them, and re-layouts  68.2 us (6%)
  other arithmetic  44.6 us (4%)
  between operations  14.8 us (1%)
    reduce_scatter x4, waiting for transfers between devices, body(): lax.psum_scatter(lax.dot_general(orthonormal, part, (((0,), (0,)), ((), (...  252 us
    all_gather x4, waiting for transfers between devices, body(): gathered.append(lax.all_gather(shares[c], 'row', axis=0, tiled=True))  193 us
    psum x1, waiting for transfers between devices, body(): packed = lax.psum(packed_gram(row_share), ('row', 'col'))  136 us
    pallas_call x1, Pallas kernels, orthonormalize(): pl.pallas_call(factor_kernel, out_shape=jax.ShapeDtypeStruct(row_share.sh...  73.5 us
    unnamed x25, local copies, waits for them, and re-layouts  68.1 us
    all_gather x1, waiting for transfers between devices, body(): lax.all_gather(right_basis, 'row', axis=0, tiled=True)  64.1 us
    reduce_scatter x1, waiting for transfers between devices, body(): lax.psum_scatter(partial_value.astype(jnp.bfloat16), 'col', scatter_dimen...  42.9 us
    dot_general x4, matrix products, body(): jnp.dot(orthonormal, gathered[c], preferred_element_type=jnp.float32)  40.3 us
  transfers between devices with their start and end apart: 12, of which 12 were waited for; matrix products, arithmetic and copies ran while one was open for 9% of the time, Pallas kernels for 0%

profile of v1, /device:TPU:0, one launch (start us, length us, event | category | flops | bytes accessed | tf_op | source)
XLA Modules:
  0.0 1063.7 jit_solution(14374595238449639032)
XLA Ops:
  7.2 0.7 all-gather.7.cloned.1.call-update
  7.9 22.6 %copy.6 = bf16[2048,4096]{0,1:T(8,128)(2,1)} copy(bf16[2048,4096]{1,0:T(8,128)(2,1)} %param.3) | data formatting | bytes 33554432 | tf_op args[0]
  30.5 22.5 %copy.7 = bf16[2048,4096]{0,1:T(8,128)(2,1)} copy(bf16[2048,4096]{1,0:T(8,128)(2,1)} %param.4) | data formatting | bytes 33554432 | tf_op args[1]
  53.0 20.3 %add_convert_fusion = bf16[2048,4096]{0,1:T(8,128)(2,1)} fusion(bf16[2048,4096]{0,1:T(8,128)(2,1)} %copy.7, bf16[2048,4096]{0,1:T(8,128)(2,1)} %copy.6), kind=kLoop, calls=%fused_computation.1 | loop fusion | flops 33554432 | bytes 50331648 | tf_op jit(solution)/shard_map/convert_element_type | solution.py:150
  73.3 64.1 %all-gather.7.cloned.1.call-done = bf16[1024,4096]{1,0:T(8,128)(2,1)} async-done(((bf16[128,4096]{1,0:T(8,128)(2,1)}), bf16[1024,4096]{1,0:T(8,128)(2,1)}) %all-gather.7.cloned.1.call-update) | async-done | bytes 8388624 | tf_op jit(solution)/shard_map/all_gather | solution.py:154
  137.3 23.9 %convolution_convert_fusion = bf16[2048,1024]{1,0:T(8,128)(2,1)} fusion(bf16[2048,4096]{0,1:T(8,128)(2,1)} %add_convert_fusion, bf16[1024,4096]{1,0:T(8,128)(2,1)} %all-gather.7.cloned.1.call-done), kind=kOutput, calls=%fused_computation.20 | convolution fusion | flops 17181966336 | bytes 29360128 | tf_op jit(solution)/shard_map/dot_general | solution.py:152
  161.2 0.0 all-reduce.2.cloned.1.call-start
  161.3 42.9 %reduce-scatter.6.cloned.1.call-done.share_ref = bf16[512,1024]{1,0:T(8,128)(2,1)} async-done(((bf16[2048,1024]{1,0:T(8,128)(2,1)}), bf16[512,1024]{1,0:T(8,128)(2,1)}) %reduce-scatter.6.cloned.1.call-update) | async-done | bytes 1048592 | tf_op jit(solution)/shard_map/reduce_scatter | solution.py:158
  204.2 1.4 fusion.36
  205.6 1.4 fusion.30
  207.0 1.7 fusion.28
  208.7 0.5 fusion.32
  209.2 1.7 pad_maximum_fusion.1
  210.9 0.3 all-gather.9.cloned.1.call-start
  211.2 136.1 %all-reduce.2.cloned.1.call-done.packed_ref = f32[256,2560]{1,0:T(8,128)} async-done(((f32[256,2560]{1,0:T(8,128)}), f32[256,2560]{1,0:T(8,128)}) %all-reduce.2.cloned.1.call-update) | async-done | bytes 2621456 | tf_op jit(solution)/shard_map/psum | solution.py:161
  347.3 1.7 copy-done.1
  349.0 73.5 %factor.1 = bf16[512,1024]{1,0:T(8,128)(2,1)} custom-call(f32[256,2560]{1,0:T(8,128)S(1)} %copy-done.1, bf16[512,1024]{1,0:T(8,128)(2,1)S(1)} %copy-done), custom_call_target="tpu_custom_call" | custom-call | tf_op jit(solution)/shard_map/factor/pallas_call | solution.py:124
  422.6 0.0 reduce-scatter.14.cloned.1.call-start
  422.6 33.4 %all-gather.9.cloned.1.call-done = bf16[2048,1024]{1,0:T(8,128)(2,1)} async-done(((bf16[512,1024]{1,0:T(8,128)(2,1)}), bf16[2048,1024]{1,0:T(8,128)(2,1)}) %all-gather.9.cloned.1.call-update) | async-done | bytes 4194320 | tf_op jit(solution)/shard_map/all_gather | solution.py:163
  456.0 9.3 fusion.25
  465.4 0.3 reduce-scatter.12.cloned.1.call-start
  465.7 9.3 fusion.22
  475.1 9.3 fusion.19
  484.4 0.5 reduce-scatter.8.cloned.1.call-start
  484.9 9.6 fusion.16
  494.6 39.3 %reduce-scatter.14.cloned.1.call-done = bf16[128,1024]{1,0:T(8,128)(2,1)} async-done(((bf16[1024,1024]{1,0:T(8,128)(2,1)}), bf16[128,1024]{1,0:T(8,128)(2,1)}) %reduce-scatter.14.cloned.1.call-update) | async-done | bytes 262160 | tf_op jit(solution)/shard_map/reduce_scatter | solution.py:169
  534.0 71.2 %reduce-scatter.12.cloned.1.call-done = bf16[128,1024]{1,0:T(8,128)(2,1)} async-done(((bf16[1024,1024]{1,0:T(8,128)(2,1)}), bf16[128,1024]{1,0:T(8,128)(2,1)}) %reduce-scatter.12.cloned.1.call-update) | async-done | bytes 262160 | tf_op jit(solution)/shard_map/reduce_scatter | solution.py:169
  605.3 70.8 %reduce-scatter.10.cloned.1.call-done = bf16[128,1024]{1,0:T(8,128)(2,1)} async-done(((bf16[1024,1024]{1,0:T(8,128)(2,1)}), bf16[128,1024]{1,0:T(8,128)(2,1)}) %reduce-scatter.10.cloned.1.call-update) | async-done | bytes 262160 | tf_op jit(solution)/shard_map/reduce_scatter | solution.py:169
  676.2 70.8 %reduce-scatter.8.cloned.1.call-done = bf16[128,1024]{1,0:T(8,128)(2,1)} async-done(((bf16[1024,1024]{1,0:T(8,128)(2,1)}), bf16[128,1024]{1,0:T(8,128)(2,1)}) %reduce-scatter.8.cloned.1.call-update) | async-done | bytes 262160 | tf_op jit(solution)/shard_map/reduce_scatter | solution.py:169
  747.0 50.3 %all-gather.17.cloned.1.call-done = bf16[1024,1024]{1,0:T(8,128)(2,1)} async-done(((bf16[128,1024]{1,0:T(8,128)(2,1)}), bf16[1024,1024]{1,0:T(8,128)(2,1)}) %all-gather.17.cloned.1.call-update) | async-done | bytes 2097168 | tf_op jit(solution)/shard_map/all_gather | solution.py:180
  797.3 2.1 multiply_reduce_fusion
  799.4 47.6 %all-gather.15.cloned.1.call-done = bf16[1024,1024]{1,0:T(8,128)(2,1)} async-done(((bf16[128,1024]{1,0:T(8,128)(2,1)}), bf16[1024,1024]{1,0:T(8,128)(2,1)}) %all-gather.15.cloned.1.call-update) | async-done | bytes 2097168 | tf_op jit(solution)/shard_map/all_gather | solution.py:180
  846.9 2.1 multiply_reduce_fusion.1
  849.0 47.7 %all-gather.13.cloned.1.call-done = bf16[1024,1024]{1,0:T(8,128)(2,1)} async-done(((bf16[128,1024]{1,0:T(8,128)(2,1)}), bf16[1024,1024]{1,0:T(8,128)(2,1)}) %all-gather.13.cloned.1.call-update) | async-done | bytes 2097168 | tf_op jit(solution)/shard_map/all_gather | solution.py:180
  896.7 2.1 multiply_reduce_fusion.2
  898.8 47.6 %all-gather.11.cloned.1.call-done = bf16[1024,1024]{1,0:T(8,128)(2,1)} async-done(((bf16[128,1024]{1,0:T(8,128)(2,1)}), bf16[1024,1024]{1,0:T(8,128)(2,1)}) %all-gather.11.cloned.1.call-update) | async-done | bytes 2097168 | tf_op jit(solution)/shard_map/all_gather | solution.py:180
  946.3 2.1 multiply_reduce_fusion.3
  948.4 5.8 psum.15
  954.3 9.1 subtract_convert_fusion.3
  963.4 11.0 %subtract_convert_fusion.2 = bf16[2048,1024]{0,1:T(8,128)(2,1)} fusion(bf16[2048,1024]{1,0:T(8,128)(2,1)} %all-gather.9.cloned.1.call-done, bf16[1024,1024]{1,0:T(8,128)(2,1)} %all-gather.13.cloned.1.call-done, bf16[2048,4096]{0,1:T(8,128)(2,1)} %add_convert_fusion), kind=kOutput, calls=%fused_computation.14 | convolution fusion | flops 4303355904 | bytes 14680064 | tf_op jit(solution)/shard_map/dot_general | solution.py:183
  974.5 10.2 subtract_convert_fusion.1
  984.7 10.0 subtract_convert_fusion
  994.6 12.5 %pad_maximum_fusion = bf16[2048,4096]{0,1:T(8,128)(2,1)} fusion(bf16[2048,1024]{0,1:T(8,128)(2,1)} %subtract_convert_fusion, bf16[2048,1024]{0,1:T(8,128)(2,1)} %subtract_convert_fusion.1, bf16[2048,1024]{0,1:T(8,128)(2,1)} %subtract_convert_fusion.2, bf16[2048,1024]{0,1:T(8,128)(2,1)S(1)} %subtract_convert_fusion.3), kind=kLoop, calls=%fused_computation.2 | loop fusion | flops 67108864 | bytes 33554432 | tf_op jit(solution)/shard_map/concatenate | solution.py:188
  1007.1 21.3 %copy.9 = bf16[2048,4096]{1,0:T(8,128)(2,1)} copy(bf16[2048,4096]{0,1:T(8,128)(2,1)} %pad_maximum_fusion) | data formatting | bytes 33554432
  1028.4 0.1 dynamic-slice.3
  1028.5 0.3 convert_multiply_fusion.3
  1028.8 1.5 pad_maximum_fusion.2
  1030.3 26.1 %multiply_convert_fusion = bf16[2048,4096]{1,0:T(8,128)(2,1)} fusion(bf16[2048,1024]{1,0:T(8,128)(2,1)} %all-gather.9.cloned.1.call-done, bf16[1024,1024]{1,0:T(8,128)(2,1)S(1)} %copy-done.2, bf16[1024,1024]{1,0:T(8,128)(2,1)} %all-gather.15.cloned.1.call-done, bf16[1024,1024]{1,0:T(8,128)(2,1)} %all-gather.13.cloned.1.call-done, ...), kind=kOutput, calls=%fused_computation | convolution fusion | flops 17238589440 | bytes 29364224 | tf_op jit(solution)/shard_map/dot_general | solution.py:196
  (42 shorter events, 0.5 us)
Async XLA Ops:
  7.2 130.2 %all-gather.7.cloned.1.call-start = ((), (), s32[]{:S(2)}) async-start(), calls=%async_computation.5 | async-start | bytes 9437184 | tf_op jit(solution)/shard_map/all_gather | solution.py:154
  7.9 196.3 %reduce-scatter.6.cloned.1.call-start = ((), (), s32[]{:S(2)}) async-start(), calls=%async_computation.6 | async-start | bytes 5242880 | tf_op jit(solution)/shard_map/reduce_scatter | solution.py:158
  161.2 186.1 %all-reduce.2.cloned.1.call-start = ((), (), s32[]{:S(2)}) async-start(), calls=%async_computation.7 | async-start | bytes 5242880 | tf_op jit(solution)/shard_map/psum | solution.py:161
  204.2 4.5 copy-start
  210.9 245.1 %all-gather.9.cloned.1.call-start = ((), (), s32[]{:S(2)}) async-start(), calls=%async_computation.8 | async-start | bytes 5242880 | tf_op jit(solution)/shard_map/all_gather | solution.py:163
  347.3 1.7 copy-start.1
  422.6 111.3 %reduce-scatter.14.cloned.1.call-start = ((), (), s32[]{:S(2)}) async-start(), calls=%async_computation.15 | async-start | bytes 2359296 | tf_op jit(solution)/shard_map/reduce_scatter | solution.py:169
  465.4 139.8 %reduce-scatter.12.cloned.1.call-start = ((), (), s32[]{:S(2)}) async-start(), calls=%async_computation.13 | async-start | bytes 2359296 | tf_op jit(solution)/shard_map/reduce_scatter | solution.py:169
  475.0 201.1 %reduce-scatter.10.cloned.1.call-start = ((), (), s32[]{:S(2)}) async-start(), calls=%async_computation.11 | async-start | bytes 2359296 | tf_op jit(solution)/shard_map/reduce_scatter | solution.py:169
  484.4 262.5 %reduce-scatter.8.cloned.1.call-start = ((), (), s32[]{:S(2)}) async-start(), calls=%async_computation.9 | async-start | bytes 2359296 | tf_op jit(solution)/shard_map/reduce_scatter | solution.py:169
  494.6 302.7 %all-gather.17.cloned.1.call-start = ((), (), s32[]{:S(2)}) async-start(), calls=%async_computation.16 | async-start | bytes 2359296 | tf_op jit(solution)/shard_map/all_gather | solution.py:180
  533.9 313.0 %all-gather.15.cloned.1.call-start = ((), (), s32[]{:S(2)}) async-start(), calls=%async_computation.14 | async-start | bytes 2359296 | tf_op jit(solution)/shard_map/all_gather | solution.py:180
  605.2 291.5 %all-gather.13.cloned.1.call-start = ((), (), s32[]{:S(2)}) async-start(), calls=%async_computation.12 | async-start | bytes 2359296 | tf_op jit(solution)/shard_map/all_gather | solution.py:180
  676.1 270.2 %all-gather.11.cloned.1.call-start = ((), (), s32[]{:S(2)}) async-start(), calls=%async_computation.10 | async-start | bytes 2359296 | tf_op jit(solution)/shard_map/all_gather | solution.py:180
  954.3 20.2 %slice-start = ((s8[16777216]{0:T(1024)(128)(4,1)}), s8[4194304]{0:T(1024)(128)(4,1)S(1)}, s32[]{:S(2)}) async-start(s8[16777216]{0:T(1024)(128)(4,1)} %bitcast.16), calls=%async_computation.17 | async-start | bytes 8388608
  954.3 20.2 %slice-start.1 = ((s8[16777216]{0:T(1024)(128)(4,1)}), s8[4194304]{0:T(1024)(128)(4,1)S(1)}, s32[]{:S(2)}) async-start(s8[16777216]{0:T(1024)(128)(4,1)} %bitcast.16), calls=%async_computation.18 | async-start | bytes 8388608
  963.4 11.1 %slice-start.2 = ((s8[16777216]{0:T(1024)(128)(4,1)}), s8[4194304]{0:T(1024)(128)(4,1)S(1)}, s32[]{:S(2)}) async-start(s8[16777216]{0:T(1024)(128)(4,1)} %bitcast.16), calls=%async_computation.19 | async-start | bytes 8388608
  963.4 11.1 %slice-start.3 = ((s8[16777216]{0:T(1024)(128)(4,1)}), s8[4194304]{0:T(1024)(128)(4,1)S(1)}, s32[]{:S(2)}) async-start(s8[16777216]{0:T(1024)(128)(4,1)} %bitcast.16), calls=%async_computation.20 | async-start | bytes 8388608
  1007.1 21.4 %copy-start.3 = (bf16[128,1024]{1,0:T(8,128)(2,1)S(1)}, bf16[128,1024]{1,0:T(8,128)(2,1)}, u32[]{:S(2)}) copy-start(bf16[128,1024]{1,0:T(8,128)(2,1)} %reduce-scatter.14.cloned.1.call-done) | copy-start | bytes 786436
  1007.1 21.4 %copy-start.4 = (bf16[128,1024]{1,0:T(8,128)(2,1)S(1)}, bf16[128,1024]{1,0:T(8,128)(2,1)}, u32[]{:S(2)}) copy-start(bf16[128,1024]{1,0:T(8,128)(2,1)} %reduce-scatter.12.cloned.1.call-done) | copy-start | bytes 786436
  1007.1 21.4 %copy-start.5 = (bf16[128,1024]{1,0:T(8,128)(2,1)S(1)}, bf16[128,1024]{1,0:T(8,128)(2,1)}, u32[]{:S(2)}) copy-start(bf16[128,1024]{1,0:T(8,128)(2,1)} %reduce-scatter.10.cloned.1.call-done) | copy-start | bytes 786436
  1007.1 21.4 %copy-start.6 = (bf16[128,1024]{1,0:T(8,128)(2,1)S(1)}, bf16[128,1024]{1,0:T(8,128)(2,1)}, u32[]{:S(2)}) copy-start(bf16[128,1024]{1,0:T(8,128)(2,1)} %reduce-scatter.8.cloned.1.call-done) | copy-start | bytes 786436
  1028.4 1.9 copy-start.2
Sparse Core Ops, SparseCore 0:
  10.1 127.1 all-gather.6
  161.3 42.7 reduce-scatter.5
  211.0 136.1 all-reduce.1
  422.7 33.3 all-gather.8
  465.5 68.3 reduce-scatter.13
  537.9 67.2 reduce-scatter.11
  608.7 67.3 reduce-scatter.9
  679.6 67.3 reduce-scatter.7
  749.1 48.1 all-gather.16
  799.3 47.6 all-gather.14
  849.1 47.6 all-gather.12
  898.7 47.6 all-gather.10
